TPU v7x, 32 devices: a whole 2x2x4 slice. The times are simulated.
32 devices in a mesh: row: 4 (over z), col: 8 (over y, x, core).
Axes of the slice: x: 2, y: 2, z: 4, core: 2. Of those that a mesh axis runs over, the one named last changes fastest.
Arguments:
- embedding: float32 [4096, 256], P(('row', 'col')), may hold values from -6 to 6
- seed_cluster: int32 [4096], P(('row', 'col')), may hold values from 0 to 127
Outputs:
- log_member: float32 [4096, 128], P(('row', 'col'))
All inputs are finite; a program needn't handle non-finite values.
Results may differ from a plain program's by a relative error of at most 0.0003.
Values sent between devices are 32-bit elements; how exact they have to be, the bound alone decides.
A program may use at most 64 MiB of HBM per device.

v0:
```python
import jax
import jax.numpy as jnp
from jax import lax
from jax.sharding import PartitionSpec as P

CLUSTER_COUNT = 128
SWEEPS = 2


ANNEAL_TEMP_VALUE = 0.02


def shards(embedding, seed_cluster):
    per_device = embedding.shape[0]
    row_coords = lax.all_gather(embedding, "col", axis=0, tiled=True)
    col_coords, col_seeds = (
        lax.all_gather(embedding, "row", axis=0, tiled=True),
        lax.all_gather(seed_cluster, "row", axis=0, tiled=True),
    )
    row_sq = jnp.sum(row_coords * row_coords, axis=1)
    col_sq = jnp.sum(col_coords * col_coords, axis=1)
    inner = jnp.dot(row_coords, col_coords.T, precision=lax.Precision.HIGHEST)
    distance = jnp.sqrt(row_sq[:, None] + col_sq[None, :] - 2.0 * inner + 1.0)
    cluster_labels = jnp.arange(CLUSTER_COUNT, dtype=jnp.int32)
    member_cols = (
        0.5 * (col_seeds[:, None] == cluster_labels[None, :]).astype(jnp.float32)
        + 0.5 / CLUSTER_COUNT
    )
    member_own = (
        0.5 * (seed_cluster[:, None] == cluster_labels[None, :]).astype(jnp.float32)
        + 0.5 / CLUSTER_COUNT
    )
    log_member = jnp.zeros((per_device, CLUSTER_COUNT), jnp.float32)
    for sweep in range(SWEEPS):
        columns = member_cols
        attraction = lax.psum_scatter(
            jnp.dot(distance, columns, precision=lax.Precision.HIGHEST),
            "col",
            scatter_dimension=0,
            tiled=True,
        )
        counts, cohesion = lax.psum(
            (jnp.sum(member_own, axis=0), jnp.sum(member_own * attraction, axis=0)), ("row", "col")
        )
        pair_energy = attraction / counts[None, :] - cohesion[None, :] / (
            2.0 * counts[None, :] ** 2
        )
        member_logits = -pair_energy / ANNEAL_TEMP_VALUE
        highest = jnp.max(member_logits, axis=1, keepdims=True)
        log_member = (
            member_logits
            - highest
            - jnp.log(jnp.sum(jnp.exp(member_logits - highest), axis=1, keepdims=True))
        )
        member_own = jnp.exp(log_member)
        if sweep + 1 < SWEEPS:
            member_cols = lax.all_gather(member_own, "row", axis=0, tiled=True)
    return log_member


def solution(mesh):
    return jax.shard_map(
        shards,
        mesh=mesh,
        in_specs=(P(("row", "col"), None), P(("row", "col"))),
        out_specs=P(("row", "col"), None),
        check_vma=False,
    )
```

profile of v0, /device:TPU:0, one launch (start us, length us, event | category | flops | bytes accessed | tf_op | source)
XLA Modules:
  0.0 222.9 jit_solution(15321643899458992196)
XLA Ops:
  6.5 0.0 all-gather.3.cloned.1.call-start
  6.5 0.7 all-gather.3.cloned.1.call-update
  7.3 0.0 reduce-scatter.3.cloned.1.call-start
  7.3 12.8 %all-gather = s32[4,1,128]{2,1,0:T(1,128)S(1)} all-gather(s32[1,1,128]{2,1,0:T(1,128)} %bitcast.8), channel_id=1, replica_groups=mesh['row'=4,'col'=8] {'row'}, dimensions={0}, use_global_device_ids=true | all-gather | bytes 2560 | tf_op jit(solution)/shard_map/all_gather | solution.py:18
  20.1 15.0 %all_gather.13 = f32[512,256]{1,0:T(8,128)S(1)} all-gather(f32[128,256]{1,0:T(8,128)} %param.2), channel_id=1, replica_groups=mesh['row'=4,'col'=8] {'row'}, dimensions={0}, use_global_device_ids=true | all-gather | bytes 655360 | tf_op jit(solution)/shard_map/all_gather | solution.py:17
  35.1 0.1 multiply_reduce_fusion.1
  35.2 0.1 all-gather.3.cloned.1.call-done
  35.3 1.4 multiply_reduce_fusion
  36.8 3.9 %add_sqrt_fusion = f32[1024,512]{1,0:T(8,128)S(1)} fusion(f32[1024,256]{1,0:T(8,128)} %all-gather.3.cloned.1.call-done, f32[512,256]{1,0:T(8,128)S(1)} %all_gather.13, f32[512]{0:T(512)S(1)} %multiply_reduce_fusion.1, f32[1024]{0:T(1024)S(1)} %multiply_reduce_fusion), kind=kOutput, calls=%fused_computation | convolution fusion | flops 1612709888 | bytes 3676160 | tf_op jit(solution)/shard_map/dot_general | solution.py:22
  40.7 0.0 copy-start.1
  40.7 2.7 %fusion = f32[1024,128]{1,0:T(8,128)} fusion(f32[1024,512]{1,0:T(8,128)S(1)} %add_sqrt_fusion, s32[512]{0:T(512)S(1)} %bitcast.7), kind=kOutput, calls=%fused_computation.3 | convolution fusion | flops 805502976 | bytes 2623488 | tf_op jit(solution)/shard_map/dot_general | solution.py:37
  43.3 0.0 reduce-scatter.3.cloned.1.call-update
  43.4 0.0 reduce-scatter.5.cloned.1.call-start
  43.4 34.2 %reduce-scatter.3.cloned.1.call-done = f32[128,128]{1,0:T(8,128)} async-done(((f32[1024,128]{1,0:T(8,128)}), f32[128,128]{1,0:T(8,128)}) %reduce-scatter.3.cloned.1.call-update) | async-done | bytes 65552 | tf_op jit(solution)/shard_map/reduce_scatter | solution.py:36
  77.6 0.0 copy-done.1
  77.6 0.0 copy-start
  77.6 1.0 fusion.7
  78.7 39.3 %all-reduce.1 = (f32[128]{0:T(128)S(1)}, f32[128]{0:T(128)S(1)}) all-reduce(f32[128]{0:T(128)S(1)} %get-tuple-element.8, f32[128]{0:T(128)S(1)} %get-tuple-element.7), channel_id=1, replica_groups=mesh['row'=4,'col'=8] {'row','col'}, use_global_device_ids=true, to_apply=%region_6.0 | all-reduce | flops 256 | bytes 2048 | tf_op jit(solution)/shard_map/psum | solution.py:42
  118.0 1.0 fusion.11
  118.9 1.0 exponential_reduce_fusion.1
  120.0 1.0 subtract_exponential_fusion
  120.9 14.4 %all_gather.15 = f32[512,128]{1,0:T(8,128)S(1)} all-gather(f32[128,128]{1,0:T(8,128)S(1)} %subtract_exponential_fusion), channel_id=1, replica_groups=mesh['row'=4,'col'=8] {'row'}, dimensions={0}, use_global_device_ids=true | all-gather | bytes 327680 | tf_op jit(solution)/shard_map/all_gather | solution.py:57
  135.3 2.6 %fusion.14 = f32[1024,128]{1,0:T(8,128)} fusion(f32[1024,512]{1,0:T(8,128)S(1)} %add_sqrt_fusion, f32[512,128]{1,0:T(8,128)S(1)} %all_gather.15), kind=kOutput, calls=%fused_computation.30 | convolution fusion | flops 805306368 | bytes 2883584 | tf_op jit(solution)/shard_map/dot_general | solution.py:37
  137.9 0.0 reduce-scatter.5.cloned.1.call-update
  137.9 34.6 %reduce-scatter.5.cloned.1.call-done = f32[128,128]{1,0:T(8,128)} async-done(((f32[1024,128]{1,0:T(8,128)}), f32[128,128]{1,0:T(8,128)}) %reduce-scatter.5.cloned.1.call-update) | async-done | bytes 65552 | tf_op jit(solution)/shard_map/reduce_scatter | solution.py:36
  172.5 0.0 copy-done
  172.5 1.0 fusion.13
  173.5 39.3 %all-reduce = (f32[128]{0:T(128)S(1)}, f32[128]{0:T(128)S(1)}) all-reduce(f32[128]{0:T(128)S(1)} %get-tuple-element.6, f32[128]{0:T(128)S(1)} %get-tuple-element.5), channel_id=1, replica_groups=mesh['row'=4,'col'=8] {'row','col'}, use_global_device_ids=true, to_apply=%region_13.0 | all-reduce | flops 256 | bytes 2048 | tf_op jit(solution)/shard_map/psum | solution.py:42
  212.8 1.0 fusion.12
  213.7 1.0 exponential_reduce_fusion
  214.8 1.6 subtract_subtract_fusion
  (4 shorter events, 0.0 us)
Async XLA Ops:
  6.5 28.8 %all-gather.3.cloned.1.call-start = ((), (), s32[]{:S(2)}) async-start(), calls=%async_computation.2 | async-start | bytes 1179648 | tf_op jit(solution)/shard_map/all_gather | solution.py:15
  7.3 70.4 %reduce-scatter.3.cloned.1.call-start = ((), (), s32[]{:S(2)}) async-start(), calls=%async_computation.3 | async-start | bytes 589824 | tf_op jit(solution)/shard_map/reduce_scatter | solution.py:36
  40.7 37.0 %copy-start.1 = (s32[128]{0:T(128)S(1)}, s32[128]{0:T(128)}, u32[]{:S(2)}) copy-start(s32[128]{0:T(128)} %param.3) | copy-start | bytes 1540
  43.4 129.1 %reduce-scatter.5.cloned.1.call-start = ((), (), s32[]{:S(2)}) async-start(), calls=%async_computation.4 | async-start | bytes 589824 | tf_op jit(solution)/shard_map/reduce_scatter | solution.py:36
  77.6 94.8 %copy-start = (f32[128,128]{1,0:T(8,128)S(1)}, f32[128,128]{1,0:T(8,128)}, u32[]{:S(2)}) copy-start(f32[128,128]{1,0:T(8,128)} %reduce-scatter.3.cloned.1.call-done) | copy-start | bytes 196612
Sparse Core Ops, SparseCore 0:
  9.2 26.0 all-gather.2
  43.5 34.1 reduce-scatter.2
  138.0 34.4 reduce-scatter.4
where the time goes:
time: 224 us; the launch traced here: 223 us
  blocking collectives  121 us (54%)
  waiting for transfers between devices  69.7 us (31%)
  between operations  13.2 us (6%)
  other arithmetic  10 us (4%)
  matrix products  9.11 us (4%)
    psum x2, blocking collectives, shards(): lax.psum((jnp.sum(member_own, axis=0), jnp.sum(member_own * attraction, a...  78.6 us
    reduce_scatter x2, waiting for transfers between devices, shards(): lax.psum_scatter(jnp.dot(distance, columns, precision=lax.Precision.HIGHE...  68.8 us
    all_gather x1, blocking collectives, shards(): lax.all_gather(embedding, 'row', axis=0, tiled=True)  15 us
    all_gather x1, blocking collectives, shards(): member_cols = lax.all_gather(member_own, 'row', axis=0, tiled=True)  14.4 us
    all_gather x1, blocking collectives, shards(): lax.all_gather(seed_cluster, 'row', axis=0, tiled=True)  12.8 us
    dot_general x2, matrix products, shards(): jnp.dot(distance, columns, precision=lax.Precision.HIGHEST)  5.25 us
  transfers between devices with their start and end apart: 3, of which 3 were waited for; matrix products, arithmetic and copies ran while one was open for 0% of the time, Pallas kernels for 0%

commit v1 on v0

v1 whole, which is shorter than its diff:
```python
import functools

import jax
import jax.numpy as jnp
from jax import lax
from jax.experimental import pallas as pl
from jax.experimental.pallas import tpu as pltpu
from jax.sharding import PartitionSpec as P

CLUSTER_COUNT = 128
SWEEPS = 2
ANNEAL_TEMP_VALUE = 0.02
MESH = pl.DeviceIdType.MESH


def flip(index, offset, size):
    out, bit = 0, 1
    while bit < size:
        out = out + bit * ((index // bit + offset // bit) % 2)
        bit *= 2
    return out


def split3(x):
    first = x.astype(jnp.bfloat16)
    rest = x - first.astype(jnp.float32)
    second = rest.astype(jnp.bfloat16)
    third = (rest - second.astype(jnp.float32)).astype(jnp.bfloat16)
    return first, second, third


def nt(a, b):
    return lax.dot_general(
        a, b, (((1,), (1,)), ((), ())), preferred_element_type=jnp.float32
    )


def nn(a, b):
    return jnp.dot(a, b, preferred_element_type=jnp.float32)


def seeds_to_member(seeds):
    points = seeds.shape[1]
    labels = lax.broadcasted_iota(jnp.int32, (CLUSTER_COUNT, points), 0)
    chosen = jnp.where(labels == seeds, 0.5, 0.0).astype(jnp.float32)
    return chosen.T + 0.5 / CLUSTER_COUNT


def kernel(
    R, C, e_ref, s_ref, o_ref,
    e_row, e_col, s_row, s_col, c1, c2, c3, csq, d1, d2, d3, m1, m2, m3, m_row,
    m_own, m_col, pp, pin, psum, rin, az_own, az_in, ac_own, ac_in,
    er_s, er_r, rel_s, rel_r, ec_s, ec_r, sr_s, sr_r, sc_s, sc_r,
    px_s, px_r, rs_s, rs_r, az_s, az_r, ac_s, ac_r,
    mz_s, mz_r, mc_s, mc_r, mrel_s, mrel_r,
):
    n = e_ref.shape[0]
    Q = C // 2
    r = lax.axis_index("row")
    c = lax.axis_index("col")
    q, b = c // 2, c % 2
    started = []

    def send(src, dst, ssem, rsem, row, col):
        copy = pltpu.make_async_remote_copy(
            src_ref=src, dst_ref=dst, send_sem=ssem, recv_sem=rsem,
            device_id=(row, col), device_id_type=MESH,
        )
        copy.start()
        started.append(copy)
        return copy

    def row_peer(t):
        return flip(r, t, R)

    def chip_peer(s):
        return flip(q, s, Q)

    def col_of(chip, core):
        return chip * 2 + core

    def rows_at(col):
        return pl.ds(pl.multiple_of(col * n, n), n)

    partner = col_of(q, 1 - b)

    barrier = pltpu.get_barrier_semaphore()
    for t in range(1, R):
        pl.semaphore_signal(barrier, inc=1, device_id=(row_peer(t), c), device_id_type=MESH)
    for u in range(1, C):
        pl.semaphore_signal(barrier, inc=1, device_id=(r, flip(c, u, C)), device_id_type=MESH)
    pl.semaphore_wait(barrier, R + C - 2)

    order_q = list(range(Q - 1, 0, -1))
    order_r = list(range(R - 1, 0, -1))
    direct = {}
    for s in order_q:
        direct[s] = send(e_ref, e_row.at[rows_at(c)], er_s.at[s], er_r.at[s], r, col_of(chip_peer(s), b))
    alongz = {}
    for t in order_r:
        alongz[t] = send(e_ref, e_col.at[rows_at(r)], ec_s.at[t], ec_r.at[t], row_peer(t), c)
    direct[0] = send(e_ref, e_row.at[rows_at(c)], er_s.at[0], er_r.at[0], r, partner)
    seeds_col = [None] + [
        send(s_ref, s_row.at[c], sr_s.at[u], sr_r.at[u], r, flip(c, u, C)) for u in range(1, C)
    ]
    seeds_rw = [None] + [
        send(s_ref, s_col.at[r], sc_s.at[t], sc_r.at[t], row_peer(t), c) for t in range(1, R)
    ]

    e_row[rows_at(c), :] = e_ref[...]
    own_member = seeds_to_member(s_ref[...])
    m_row[rows_at(c), :] = own_member

    def ready_column(x, row):
        at = rows_at(row)
        p1, p2, p3 = split3(x)
        c1[at, :] = p1
        c2[at, :] = p2
        c3[at, :] = p3
        q1, q2, q3 = split3(x * x)
        ones = jnp.ones((8, x.shape[1]), jnp.bfloat16)
        csq[:, at] = (nt(ones, q3) + nt(ones, q2)) + nt(ones, q1)

    ready_column(e_ref[...], r)
    m1[rows_at(r), :] = own_member.astype(jnp.bfloat16)

    for u in range(1, C):
        seeds_col[u].wait_recv()
        col = flip(c, u, C)
        m_row[rows_at(col), :] = seeds_to_member(s_row[col])
    for t in range(1, R):
        seeds_rw[t].wait_recv()
        row = row_peer(t)
        m1[rows_at(row), :] = seeds_to_member(s_col[row]).astype(jnp.bfloat16)

    relay = {}

    def forward(s):
        direct[s].wait_recv()
        at = rows_at(col_of(chip_peer(s), b))
        relay[s] = send(e_row.at[at], e_row.at[at], rel_s.at[s], rel_r.at[s], r, partner)

    for i in range(1, max(Q, R)):
        if i < R:
            alongz[i].wait_recv()
            row = row_peer(i)
            ready_column(e_col[rows_at(row), :], row)
        if i < Q:
            forward(i)

    def make_distance(s):
        if s == 0:
            direct[0].wait_recv()
        else:
            relay[s].wait_recv()
        pair = pl.ds(pl.multiple_of(chip_peer(s) * (2 * n), 2 * n), 2 * n)
        x = e_row[pair, :]
        x1, x2, x3 = split3(x)
        inner = nt(x3, c1[...]) + nt(x2, c2[...]) + nt(x1, c3[...])
        inner = inner + (nt(x2, c1[...]) + nt(x1, c2[...]))
        inner = inner + nt(x1, c1[...])
        sq = jnp.sum(x * x, axis=1, keepdims=True)
        distance = jnp.sqrt(sq + csq[0:1, :] - 2.0 * inner + 1.0)
        p1, p2, p3 = split3(distance)
        d1[pair, :] = p1
        d2[pair, :] = p2
        d3[pair, :] = p3
        return (nn(p3, m1[...]) + nn(p2, m1[...])) + nn(p1, m1[...])

    def take_distance(s):
        pair = pl.ds(pl.multiple_of(chip_peer(s) * (2 * n), 2 * n), 2 * n)
        p1, p2, p3 = d1[pair, :], d2[pair, :], d3[pair, :]
        low = nn(p3, m1[...]) + nn(p2, m2[...]) + nn(p1, m3[...])
        mid = nn(p2, m1[...]) + nn(p1, m2[...])
        return low + mid + nn(p1, m1[...])

    log_member = None
    for w in range(SWEEPS):
        order = list(range(Q)) if w == 0 else list(range(Q - 1, -1, -1))
        exchange, scatter = {}, {}

        def combine(s):
            exchange[s].wait_recv()
            psum[w, s] = pp[w, s, b] + pin[w, s]
            if s:
                scatter[s] = send(
                    psum.at[w, s], rin.at[w, s], rs_s.at[w, s], rs_r.at[w, s],
                    r, col_of(chip_peer(s), b),
                )

        cohesion = jnp.zeros((1, CLUSTER_COUNT), jnp.float32)
        if w == 0:
            products = lambda s: make_distance(s)
        else:
            products = lambda s: take_distance(s)
        last = None
        for s in order:
            part = products(s)
            pp[w, s, 0] = part[:n]
            pp[w, s, 1] = part[n:]
            exchange[s] = send(
                pp.at[w, s, 1 - b], pin.at[w, s], px_s.at[w, s], px_r.at[w, s], r, partner
            )
            if w == 0:
                pair = pl.ds(pl.multiple_of(chip_peer(s) * (2 * n), 2 * n), 2 * n)
                cohesion = cohesion + jnp.sum(m_row[pair, :] * part, axis=0, keepdims=True)
            if last is not None:
                combine(last)
            last = s
        if w:
            for s in range(Q):
                (mc[0] if s == 0 else mrel[s]).wait_recv()
            for s in range(Q):
                pair = pl.ds(pl.multiple_of(chip_peer(s) * (2 * n), 2 * n), 2 * n)
                both = jnp.concatenate([pp[w, s, 0], pp[w, s, 1]], axis=0)
                cohesion = cohesion + jnp.sum(m_row[pair, :] * both, axis=0, keepdims=True)

        counts = jnp.sum(own_member, axis=0, keepdims=True)
        az_own[w, 0:1, :] = counts
        az_own[w, 1:2, :] = cohesion
        first = [
            send(az_own.at[w], az_in.at[w, t], az_s.at[w, t], az_r.at[w, t], row_peer(t), c)
            for t in range(1, R)
        ]
        combine(last)
        sums = az_own[w]
        for t in range(1, R):
            first[t - 1].wait_recv()
            sums = sums + az_in[w, t]
        ac_own[w] = sums
        second = [
            send(ac_own.at[w], ac_in.at[w, u], ac_s.at[w, u], ac_r.at[w, u], r, flip(c, u, C))
            for u in range(1, C)
        ]
        attraction = psum[w, 0]
        for s in order:
            if s:
                scatter[s].wait_recv()
                attraction = attraction + rin[w, s]
        for u in range(1, C):
            second[u - 1].wait_recv()
            sums = sums + ac_in[w, u]
        counts, cohesion = sums[0:1, :], sums[1:2, :]
        pair_energy = attraction / counts - cohesion / (2.0 * counts * counts)
        logits = -pair_energy / ANNEAL_TEMP_VALUE
        highest = jnp.max(logits, axis=1, keepdims=True)
        total = jnp.sum(jnp.exp(logits - highest), axis=1, keepdims=True)
        log_member = logits - highest - jnp.log(total)
        if w + 1 < SWEEPS:
            own_member = jnp.exp(log_member)
            m_own[...] = own_member
            mz, mc, mrel = {}, {}, {}
            for t in order_r:
                mz[t] = send(m_own, m_col.at[rows_at(r)], mz_s.at[t], mz_r.at[t], row_peer(t), c)
            for s in order_q:
                mc[s] = send(m_own, m_row.at[rows_at(c)], mc_s.at[s], mc_r.at[s], r, col_of(chip_peer(s), b))
            mc[0] = send(m_own, m_row.at[rows_at(c)], mc_s.at[0], mc_r.at[0], r, partner)
            m_row[rows_at(c), :] = own_member

            def ready_member(x, row):
                at = rows_at(row)
                p1, p2, p3 = split3(x)
                m1[at, :] = p1
                m2[at, :] = p2
                m3[at, :] = p3

            ready_member(own_member, r)
            for i in range(1, max(Q, R)):
                if i < R:
                    mz[i].wait_recv()
                    ready_member(m_col[rows_at(row_peer(i)), :], row_peer(i))
                if i < Q:
                    mc[i].wait_recv()
                    at = rows_at(col_of(chip_peer(i), b))
                    mrel[i] = send(m_row.at[at], m_row.at[at], mrel_s.at[i], mrel_r.at[i], r, partner)

    o_ref[...] = log_member
    for copy in started:
        copy.wait_send()


def shards(R, C, embedding, seed_cluster):
    n, features = embedding.shape
    k = CLUSTER_COUNT
    Q = C // 2
    f32, bf16, i32 = jnp.float32, jnp.bfloat16, jnp.int32
    dma = pltpu.SemaphoreType.DMA
    V = pltpu.VMEM
    return pl.pallas_call(
        functools.partial(kernel, R, C),
        out_shape=jax.ShapeDtypeStruct((n, k), f32),
        in_specs=[pl.BlockSpec(memory_space=pltpu.VMEM)] * 2,
        out_specs=pl.BlockSpec(memory_space=pltpu.VMEM),
        scratch_shapes=[
            V((C * n, features), f32), V((R * n, features), f32),
            V((C, 1, n), i32), V((R, 1, n), i32),
            V((R * n, features), bf16), V((R * n, features), bf16), V((R * n, features), bf16),
            V((8, R * n), f32),
            V((C * n, R * n), bf16), V((C * n, R * n), bf16), V((C * n, R * n), bf16),
            V((R * n, k), bf16), V((R * n, k), bf16), V((R * n, k), bf16),
            V((C * n, k), f32),
            V((n, k), f32), V((R * n, k), f32),
            V((SWEEPS, Q, 2, n, k), f32), V((SWEEPS, Q, n, k), f32),
            V((SWEEPS, Q, n, k), f32), V((SWEEPS, Q, n, k), f32),
            V((SWEEPS, 2, k), f32), V((SWEEPS, R, 2, k), f32),
            V((SWEEPS, 2, k), f32), V((SWEEPS, C, 2, k), f32),
            dma((Q,)), dma((Q,)), dma((Q,)), dma((Q,)), dma((R,)), dma((R,)),
            dma((C,)), dma((C,)), dma((R,)), dma((R,)),
            dma((SWEEPS, Q)), dma((SWEEPS, Q)), dma((SWEEPS, Q)), dma((SWEEPS, Q)),
            dma((SWEEPS, R)), dma((SWEEPS, R)), dma((SWEEPS, C)), dma((SWEEPS, C)),
            dma((R,)), dma((R,)), dma((Q,)), dma((Q,)), dma((Q,)), dma((Q,)),
        ],
        compiler_params=pltpu.CompilerParams(
            collective_id=0, has_side_effects=True, vmem_limit_bytes=60 * 1024 * 1024
        ),
    )(embedding, seed_cluster.reshape(1, n))


def solution(mesh):
    return jax.shard_map(
        functools.partial(shards, mesh.shape["row"], mesh.shape["col"]),
        mesh=mesh,
        in_specs=(P(("row", "col"), None), P(("row", "col"))),
        out_specs=P(("row", "col"), None),
        check_vma=False,
    )
```

time: 224 us -> 53.2 us (0.24)
  blocking collectives: 121 us -> 0 us
  waiting for transfers between devices: 69.7 us -> 0 us
  Pallas kernels: 0 us -> 51.5 us
  between operations: 13.2 us -> 0.01 us
  other arithmetic: 10 us -> 0 us
  matrix products: 9.11 us -> 0 us
    psum x2 -> x0, blocking collectives: 78.6 us -> none  [shards(): lax.psum((jnp.sum(member_own, axis=0), jnp.sum(member_own * attraction, a...]
    reduce_scatter x2 -> x0, waiting for transfers between devices: 68.8 us -> none  [shards(): lax.psum_scatter(jnp.dot(distance, columns, precision=lax.Precision.HIGHE...]
    pallas_call x0 -> x1, Pallas kernels: none -> 51.5 us  [shards(): pl.pallas_call(functools.partial(kernel, R, C), out_shape=jax.ShapeDtypeS...]
    all_gather x3 -> x0, blocking collectives: 42.2 us -> none  [the longest x1 15 us: shards(): lax.all_gather(embedding, 'row', axis=0, tiled=True)]
    dot_general x3 -> x0, matrix products: 9.11 us -> none  [the longest x2 5.25 us: shards(): jnp.dot(distance, columns, precision=lax.Precision.HIGHEST)]
    reduce_sum x6 -> x0, other arithmetic: 5.6 us -> none  [the longest x2 2.05 us: shards(): jnp.sum(jnp.exp(member_logits - highest), axis=1, keepdims=True)]
  transfers between devices with their start and end apart: 3 -> 0, of which waited for: 3 -> 0; matrix products, arithmetic and copies ran while one was open for 0% -> 0% of each run, Pallas kernels for 0% -> 0%
where the time goes in v1:
time: 53.2 us; the launch traced here: 53 us
  Pallas kernels  51.5 us (97%)
  local copies, waits for them, and re-layouts  1.47 us (3%)
    pallas_call x1, Pallas kernels, shards(): pl.pallas_call(functools.partial(kernel, R, C), out_shape=jax.ShapeDtypeS...  51.5 us
    unnamed x1, local copies, waits for them, and re-layouts  1.47 us

profile of v1, /device:TPU:0, one launch (start us, length us, event | category | flops | bytes accessed | tf_op | source)
XLA Modules:
  0.0 53.0 jit_solution(14627382496915632762)
XLA Ops:
  0.0 51.5 %shard_map.28 = f32[128,128]{1,0:T(8,128)} custom-call(f32[128,256]{1,0:T(8,128)} %e_ref.1, s32[1,128]{1,0:T(1,128)} %bitcast.1), custom_call_target="tpu_custom_call" | custom-call | tf_op jit(solution)/shard_map/pallas_call | solution.py:289
  51.5 1.5 %copy.4 = f32[128,128]{1,0:T(8,128)} copy(f32[128,128]{1,0:T(8,128)} %shard_map.28) | data formatting | bytes 131072

commit v2 on v1

v2 whole, which is shorter than its diff:
```python
import functools

import jax
import jax.numpy as jnp
from jax import lax
from jax.experimental import pallas as pl
from jax.experimental.pallas import tpu as pltpu
from jax.sharding import PartitionSpec as P

CLUSTER_COUNT = 128
SWEEPS = 2
ANNEAL_TEMP_VALUE = 0.02
MESH = pl.DeviceIdType.MESH


def flip(index, offset, size):
    out, bit = 0, 1
    while bit < size:
        out = out + bit * ((index // bit + offset // bit) % 2)
        bit *= 2
    return out


def split3(x):
    first = x.astype(jnp.bfloat16)
    rest = x - first.astype(jnp.float32)
    second = rest.astype(jnp.bfloat16)
    third = (rest - second.astype(jnp.float32)).astype(jnp.bfloat16)
    return first, second, third


def nt(a, b):
    return lax.dot_general(
        a, b, (((1,), (1,)), ((), ())), preferred_element_type=jnp.float32
    )


def nn(a, b):
    return jnp.dot(a, b, preferred_element_type=jnp.float32)


def seeds_to_member(seeds):
    points = seeds.shape[1]
    labels = lax.broadcasted_iota(jnp.int32, (CLUSTER_COUNT, points), 0)
    chosen = jnp.where(labels == seeds, 0.5, 0.0).astype(jnp.float32)
    return chosen.T + 0.5 / CLUSTER_COUNT


def kernel(
    R, C, e_ref, s_ref, o_ref,
    e_row, e_col, s_row, s_col, c1, c2, c3, csq, d1, d2, d3, m1, m2, m3, m_row,
    m_own, m_col, pp, pin, psum, rin, az_own, az_in, ac_own, ac_in, acc,
    er_s, er_r, rel_s, rel_r, ec_s, ec_r, sr_s, sr_r, sc_s, sc_r,
    px_s, px_r, rs_s, rs_r, az_s, az_r, ac_s, ac_r,
    mz_s, mz_r, mc_s, mc_r, mrel_s, mrel_r,
):
    n = e_ref.shape[0]
    Q = C // 2
    r = lax.axis_index("row")
    c = lax.axis_index("col")
    q, b = c // 2, c % 2
    started = []

    def send(src, dst, ssem, rsem, row, col):
        copy = pltpu.make_async_remote_copy(
            src_ref=src, dst_ref=dst, send_sem=ssem, recv_sem=rsem,
            device_id=(row, col), device_id_type=MESH,
        )
        copy.start()
        started.append(copy)
        return copy

    def row_peer(t):
        return flip(r, t, R)

    def chip_peer(s):
        return flip(q, s, Q)

    def col_of(chip, core):
        return chip * 2 + core

    def block(i):
        return pl.ds(i * n, n) if isinstance(i, int) else pl.ds(pl.multiple_of(i * n, n), n)

    def row_slot(s, core):
        return block(2 * s + core)

    def pair_slot(s):
        return pl.ds(2 * s * n, 2 * n)

    partner = col_of(q, 1 - b)
    group = 2 if R % 2 == 0 else 1
    groups = [list(range(g, g + group)) for g in range(0, R, group)]
    near_first = [1] + list(range(R - 1, 1, -1)) if R > 1 else []

    barrier = pltpu.get_barrier_semaphore()
    for t in range(1, R):
        pl.semaphore_signal(barrier, inc=1, device_id=(row_peer(t), c), device_id_type=MESH)
    for u in range(1, C):
        pl.semaphore_signal(barrier, inc=1, device_id=(r, flip(c, u, C)), device_id_type=MESH)

    def ready_column(x, t):
        at = block(t)
        p1, p2, p3 = split3(x)
        c1[at, :] = p1
        c2[at, :] = p2
        c3[at, :] = p3
        q1, q2, q3 = split3(x * x)
        ones = jnp.ones((8, x.shape[1]), jnp.bfloat16)
        csq[:, at] = (nt(ones, q3) + nt(ones, q2)) + nt(ones, q1)

    e_row[row_slot(0, b), :] = e_ref[...]
    own_member = seeds_to_member(s_ref[...])
    m_row[row_slot(0, b), :] = own_member
    m1[block(0), :] = own_member.astype(jnp.bfloat16)
    ready_column(e_ref[...], 0)

    pl.semaphore_wait(barrier, R + C - 2)

    direct, alongz = {}, {}
    for t in near_first:
        alongz[t] = send(e_ref, e_col.at[block(t)], ec_s.at[t], ec_r.at[t], row_peer(t), c)
    for s in range(Q - 1, 0, -1):
        direct[s] = send(
            e_ref, e_row.at[row_slot(s, b)], er_s.at[s], er_r.at[s], r, col_of(chip_peer(s), b)
        )
    direct[0] = send(e_ref, e_row.at[row_slot(0, b)], er_s.at[0], er_r.at[0], r, partner)
    seeds_col = {}
    for s in range(Q):
        for o in range(2):
            if s or o:
                seeds_col[s, o] = send(
                    s_ref, s_row.at[2 * s + b], sr_s.at[2 * s + o], sr_r.at[2 * s + o],
                    r, col_of(chip_peer(s), (b + o) % 2),
                )
    seeds_rw = {}
    for t in range(1, R):
        seeds_rw[t] = send(s_ref, s_col.at[t], sc_s.at[t], sc_r.at[t], row_peer(t), c)

    for s, o in seeds_col:
        seeds_col[s, o].wait_recv()
        core = (b + o) % 2
        m_row[row_slot(s, core), :] = seeds_to_member(s_row[2 * s + core])
    for t in range(1, R):
        seeds_rw[t].wait_recv()
        m1[block(t), :] = seeds_to_member(s_col[t]).astype(jnp.bfloat16)

    relay = {}
    for s in range(1, Q):
        direct[s].wait_recv()
        at = row_slot(s, b)
        relay[s] = send(e_row.at[at], e_row.at[at], rel_s.at[s], rel_r.at[s], r, partner)

    def span(ts):
        return pl.ds(ts[0] * n, len(ts) * n)

    def make_distance(s, ts):
        pair, cols = pair_slot(s), span(ts)
        x = e_row[pair, :]
        x1, x2, x3 = split3(x)
        k1, k2, k3 = c1[cols, :], c2[cols, :], c3[cols, :]
        inner = nt(x3, k1) + nt(x2, k2) + nt(x1, k3)
        inner = inner + (nt(x2, k1) + nt(x1, k2))
        inner = inner + nt(x1, k1)
        sq = jnp.sum(x * x, axis=1, keepdims=True)
        distance = jnp.sqrt(sq + csq[0:1, cols] - 2.0 * inner + 1.0)
        p1, p2, p3 = split3(distance)
        d1[pair, cols] = p1
        d2[pair, cols] = p2
        d3[pair, cols] = p3
        a1 = m1[cols, :]
        return (nn(p3, a1) + nn(p2, a1)) + nn(p1, a1)

    def take_distance(s, ts):
        pair, cols = pair_slot(s), span(ts)
        p1, p2, p3 = d1[pair, cols], d2[pair, cols], d3[pair, cols]
        a1, a2, a3 = m1[cols, :], m2[cols, :], m3[cols, :]
        low = nn(p3, a1) + nn(p2, a2) + nn(p1, a3)
        return low + (nn(p2, a1) + nn(p1, a2)) + nn(p1, a1)

    log_member = None
    mz, mc, mrel = {}, {}, {}
    for w in range(SWEEPS):
        order = list(range(Q - 1, -1, -1))
        exchange, scatter = {}, {}

        def combine(s):
            exchange[s].wait_recv()
            psum[w, s] = pp[w, s, b] + pin[w, s]
            if s:
                scatter[s] = send(
                    psum.at[w, s], rin.at[w, s], rs_s.at[w, s], rs_r.at[w, s],
                    r, col_of(chip_peer(s), b),
                )

        cohesion = jnp.zeros((1, CLUSTER_COUNT), jnp.float32)
        products = make_distance if w == 0 else take_distance
        last = None
        for at, ts in enumerate(groups):
            for t in sorted(ts, reverse=True):
                if t == 0:
                    continue
                if w == 0:
                    alongz[t].wait_recv()
                    ready_column(e_col[block(t), :], t)
                else:
                    mz[t].wait_recv()
                    ready_member(m_col[block(t), :], t)
            final = at + 1 == len(groups)
            for s in (range(Q) if at == 0 else order):
                if at == 0 and w == 0:
                    (direct[0] if s == 0 else relay[s]).wait_recv()
                part = products(s, ts)
                if at:
                    part = part + acc[s]
                if not final:
                    acc[s] = part
                    continue
                pp[w, s, 0] = part[:n]
                pp[w, s, 1] = part[n:]
                exchange[s] = send(
                    pp.at[w, s, 1 - b], pin.at[w, s], px_s.at[w, s], px_r.at[w, s], r, partner
                )
                if w:
                    (mc[0] if s == 0 else mrel[s]).wait_recv()
                cohesion = cohesion + jnp.sum(
                    m_row[pair_slot(s), :] * part, axis=0, keepdims=True
                )
                if last is not None:
                    combine(last)
                last = s
            if w and at == 0:
                for s in range(1, Q):
                    mc[s].wait_recv()
                    slot = row_slot(s, b)
                    mrel[s] = send(m_row.at[slot], m_row.at[slot], mrel_s.at[s], mrel_r.at[s], r, partner)

        counts = jnp.sum(own_member, axis=0, keepdims=True)
        az_own[w, 0:1, :] = counts
        az_own[w, 1:2, :] = cohesion
        first = [
            send(az_own.at[w], az_in.at[w, t], az_s.at[w, t], az_r.at[w, t], row_peer(t), c)
            for t in range(1, R)
        ]
        combine(last)
        sums = az_own[w]
        for t in range(1, R):
            first[t - 1].wait_recv()
            sums = sums + az_in[w, t]
        ac_own[w] = sums
        second = [
            send(ac_own.at[w], ac_in.at[w, u], ac_s.at[w, u], ac_r.at[w, u], r, flip(c, u, C))
            for u in range(1, C)
        ]
        attraction = psum[w, 0]
        for s in order:
            if s:
                scatter[s].wait_recv()
                attraction = attraction + rin[w, s]
        for u in range(1, C):
            second[u - 1].wait_recv()
            sums = sums + ac_in[w, u]
        counts, cohesion = sums[0:1, :], sums[1:2, :]
        pair_energy = attraction / counts - cohesion / (2.0 * counts * counts)
        logits = -pair_energy / ANNEAL_TEMP_VALUE
        highest = jnp.max(logits, axis=1, keepdims=True)
        total = jnp.sum(jnp.exp(logits - highest), axis=1, keepdims=True)
        log_member = logits - highest - jnp.log(total)
        if w + 1 < SWEEPS:
            own_member = jnp.exp(log_member)
            m_own[...] = own_member
            for t in near_first:
                mz[t] = send(m_own, m_col.at[block(t)], mz_s.at[t], mz_r.at[t], row_peer(t), c)
            for s in range(Q - 1, 0, -1):
                mc[s] = send(
                    m_own, m_row.at[row_slot(s, b)], mc_s.at[s], mc_r.at[s], r, col_of(chip_peer(s), b)
                )
            mc[0] = send(m_own, m_row.at[row_slot(0, b)], mc_s.at[0], mc_r.at[0], r, partner)
            m_row[row_slot(0, b), :] = own_member

            def ready_member(x, t):
                at = block(t)
                p1, p2, p3 = split3(x)
                m1[at, :] = p1
                m2[at, :] = p2
                m3[at, :] = p3

            ready_member(own_member, 0)

    o_ref[...] = log_member
    for copy in started:
        copy.wait_send()


def shards(R, C, embedding, seed_cluster):
    n, features = embedding.shape
    k = CLUSTER_COUNT
    Q = C // 2
    f32, bf16, i32 = jnp.float32, jnp.bfloat16, jnp.int32
    dma = pltpu.SemaphoreType.DMA
    V = pltpu.VMEM
    return pl.pallas_call(
        functools.partial(kernel, R, C),
        out_shape=jax.ShapeDtypeStruct((n, k), f32),
        in_specs=[pl.BlockSpec(memory_space=pltpu.VMEM)] * 2,
        out_specs=pl.BlockSpec(memory_space=pltpu.VMEM),
        scratch_shapes=[
            V((C * n, features), f32), V((R * n, features), f32),
            V((C, 1, n), i32), V((R, 1, n), i32),
            V((R * n, features), bf16), V((R * n, features), bf16), V((R * n, features), bf16),
            V((8, R * n), f32),
            V((C * n, R * n), bf16), V((C * n, R * n), bf16), V((C * n, R * n), bf16),
            V((R * n, k), bf16), V((R * n, k), bf16), V((R * n, k), bf16),
            V((C * n, k), f32),
            V((n, k), f32), V((R * n, k), f32),
            V((SWEEPS, Q, 2, n, k), f32), V((SWEEPS, Q, n, k), f32),
            V((SWEEPS, Q, n, k), f32), V((SWEEPS, Q, n, k), f32),
            V((SWEEPS, 2, k), f32), V((SWEEPS, R, 2, k), f32),
            V((SWEEPS, 2, k), f32), V((SWEEPS, C, 2, k), f32),
            V((Q, 2 * n, k), f32),
            dma((Q,)), dma((Q,)), dma((Q,)), dma((Q,)), dma((R,)), dma((R,)),
            dma((C,)), dma((C,)), dma((R,)), dma((R,)),
            dma((SWEEPS, Q)), dma((SWEEPS, Q)), dma((SWEEPS, Q)), dma((SWEEPS, Q)),
            dma((SWEEPS, R)), dma((SWEEPS, R)), dma((SWEEPS, C)), dma((SWEEPS, C)),
            dma((R,)), dma((R,)), dma((Q,)), dma((Q,)), dma((Q,)), dma((Q,)),
        ],
        compiler_params=pltpu.CompilerParams(
            collective_id=0, has_side_effects=True, vmem_limit_bytes=60 * 1024 * 1024
        ),
    )(embedding, seed_cluster.reshape(1, n))


def solution(mesh):
    return jax.shard_map(
        functools.partial(shards, mesh.shape["row"], mesh.shape["col"]),
        mesh=mesh,
        in_specs=(P(("row", "col"), None), P(("row", "col"))),
        out_specs=P(("row", "col"), None),
        check_vma=False,
    )
```

time: 53.2 us -> 55.2 us (1.038)
  Pallas kernels: 51.5 us -> 53.5 us
    pallas_call x1, Pallas kernels: 51.5 us -> 53.5 us  [shards(): pl.pallas_call(functools.partial(kernel, R, C), out_shape=jax.ShapeDtypeS...]
where the time goes in v2:
time: 55.2 us; the launch traced here: 55 us
  Pallas kernels  53.5 us (97%)
  local copies, waits for them, and re-layouts  1.47 us (3%)
    pallas_call x1, Pallas kernels, shards(): pl.pallas_call(functools.partial(kernel, R, C), out_shape=jax.ShapeDtypeS...  53.5 us
    unnamed x1, local copies, waits for them, and re-layouts  1.47 us

profile of v2, /device:TPU:0, one launch (start us, length us, event | category | flops | bytes accessed | tf_op | source)
XLA Modules:
  0.0 55.0 jit_solution(15856263561549872161)
XLA Ops:
  0.0 53.5 %shard_map.28 = f32[128,128]{1,0:T(8,128)} custom-call(f32[128,256]{1,0:T(8,128)} %e_ref.1, s32[1,128]{1,0:T(1,128)} %bitcast.1), custom_call_target="tpu_custom_call" | custom-call | tf_op jit(solution)/shard_map/pallas_call | solution.py:302
  53.5 1.5 %copy.4 = f32[128,128]{1,0:T(8,128)} copy(f32[128,128]{1,0:T(8,128)} %shard_map.28) | data formatting | bytes 131072

commit v3 on v2

--- a/solution.py
+++ b/solution.py
@@ -49,9 +49,9 @@
 def kernel(
     R, C, e_ref, s_ref, o_ref,
     e_row, e_col, s_row, s_col, c1, c2, c3, csq, d1, d2, d3, m1, m2, m3, m_row,
-    m_own, m_col, pp, pin, psum, rin, az_own, az_in, ac_own, ac_in, acc,
+    m_own, m_col, pp, pin, psum, rin, az_own, az_in, acc,
     er_s, er_r, rel_s, rel_r, ec_s, ec_r, sr_s, sr_r, sc_s, sc_r,
-    px_s, px_r, rs_s, rs_r, az_s, az_r, ac_s, ac_r,
+    px_s, px_r, rs_s, rs_r, az_s, az_r,
     mz_s, mz_r, mc_s, mc_r, mrel_s, mrel_r,
 ):
     n = e_ref.shape[0]
@@ -117,6 +117,18 @@
 
     pl.semaphore_wait(barrier, R + C - 2)
 
+    seeds_col = {}
+    for s in range(Q):
+        for o in range(2):
+            if s or o:
+                seeds_col[s, o] = send(
+                    s_ref, s_row.at[2 * s + b], sr_s.at[2 * s + o], sr_r.at[2 * s + o],
+                    r, col_of(chip_peer(s), (b + o) % 2),
+                )
+    seeds_rw = {}
+    for t in range(1, R):
+        seeds_rw[t] = send(s_ref, s_col.at[t], sc_s.at[t], sc_r.at[t], row_peer(t), c)
+
     direct, alongz = {}, {}
     for t in near_first:
         alongz[t] = send(e_ref, e_col.at[block(t)], ec_s.at[t], ec_r.at[t], row_peer(t), c)
@@ -125,17 +137,6 @@
             e_ref, e_row.at[row_slot(s, b)], er_s.at[s], er_r.at[s], r, col_of(chip_peer(s), b)
         )
     direct[0] = send(e_ref, e_row.at[row_slot(0, b)], er_s.at[0], er_r.at[0], r, partner)
-    seeds_col = {}
-    for s in range(Q):
-        for o in range(2):
-            if s or o:
-                seeds_col[s, o] = send(
-                    s_ref, s_row.at[2 * s + b], sr_s.at[2 * s + o], sr_r.at[2 * s + o],
-                    r, col_of(chip_peer(s), (b + o) % 2),
-                )
-    seeds_rw = {}
-    for t in range(1, R):
-        seeds_rw[t] = send(s_ref, s_col.at[t], sc_s.at[t], sc_r.at[t], row_peer(t), c)
 
     for s, o in seeds_col:
         seeds_col[s, o].wait_recv()
@@ -238,28 +239,25 @@
         counts = jnp.sum(own_member, axis=0, keepdims=True)
         az_own[w, 0:1, :] = counts
         az_own[w, 1:2, :] = cohesion
-        first = [
-            send(az_own.at[w], az_in.at[w, t], az_s.at[w, t], az_r.at[w, t], row_peer(t), c)
-            for t in range(1, R)
-        ]
+        shares = {}
+        for t in range(R - 1, -1, -1):
+            for u in range(C - 1, -1, -1):
+                if t or u:
+                    i = t * C + u
+                    shares[i] = send(
+                        az_own.at[w], az_in.at[w, i], az_s.at[w, i], az_r.at[w, i],
+                        row_peer(t), flip(c, u, C),
+                    )
         combine(last)
-        sums = az_own[w]
-        for t in range(1, R):
-            first[t - 1].wait_recv()
-            sums = sums + az_in[w, t]
-        ac_own[w] = sums
-        second = [
-            send(ac_own.at[w], ac_in.at[w, u], ac_s.at[w, u], ac_r.at[w, u], r, flip(c, u, C))
-            for u in range(1, C)
-        ]
         attraction = psum[w, 0]
         for s in order:
             if s:
                 scatter[s].wait_recv()
                 attraction = attraction + rin[w, s]
-        for u in range(1, C):
-            second[u - 1].wait_recv()
-            sums = sums + ac_in[w, u]
+        for i in shares:
+            shares[i].wait_recv()
+        az_in[w, 0] = az_own[w]
+        sums = jnp.sum(az_in[w], axis=0)
         counts, cohesion = sums[0:1, :], sums[1:2, :]
         pair_energy = attraction / counts - cohesion / (2.0 * counts * counts)
         logits = -pair_energy / ANNEAL_TEMP_VALUE
@@ -315,13 +313,12 @@
             V((n, k), f32), V((R * n, k), f32),
             V((SWEEPS, Q, 2, n, k), f32), V((SWEEPS, Q, n, k), f32),
             V((SWEEPS, Q, n, k), f32), V((SWEEPS, Q, n, k), f32),
-            V((SWEEPS, 2, k), f32), V((SWEEPS, R, 2, k), f32),
-            V((SWEEPS, 2, k), f32), V((SWEEPS, C, 2, k), f32),
+            V((SWEEPS, 2, k), f32), V((SWEEPS, R * C, 2, k), f32),
             V((Q, 2 * n, k), f32),
             dma((Q,)), dma((Q,)), dma((Q,)), dma((Q,)), dma((R,)), dma((R,)),
             dma((C,)), dma((C,)), dma((R,)), dma((R,)),
             dma((SWEEPS, Q)), dma((SWEEPS, Q)), dma((SWEEPS, Q)), dma((SWEEPS, Q)),
-            dma((SWEEPS, R)), dma((SWEEPS, R)), dma((SWEEPS, C)), dma((SWEEPS, C)),
+            dma((SWEEPS, R * C)), dma((SWEEPS, R * C)),
             dma((R,)), dma((R,)), dma((Q,)), dma((Q,)), dma((Q,)), dma((Q,)),
         ],
         compiler_params=pltpu.CompilerParams(

time: 55.2 us -> 47.3 us (0.86)
  Pallas kernels: 53.5 us -> 45.7 us
    pallas_call x1, Pallas kernels: 53.5 us -> 45.7 us  [shards(): pl.pallas_call(functools.partial(kernel, R, C), out_shape=jax.ShapeDtypeS...]
where the time goes in v3:
time: 47.3 us; the launch traced here: 47.2 us
  Pallas kernels  45.7 us (97%)
  local copies, waits for them, and re-layouts  1.47 us (3%)
    pallas_call x1, Pallas kernels, shards(): pl.pallas_call(functools.partial(kernel, R, C), out_shape=jax.ShapeDtypeS...  45.7 us
    unnamed x1, local copies, waits for them, and re-layouts  1.47 us

profile of v3, /device:TPU:0, one launch (start us, length us, event | category | flops | bytes accessed | tf_op | source)
XLA Modules:
  0.0 47.2 jit_solution(9107587520524160158)
XLA Ops:
  0.0 45.7 %shard_map.28 = f32[128,128]{1,0:T(8,128)} custom-call(f32[128,256]{1,0:T(8,128)} %e_ref.1, s32[1,128]{1,0:T(1,128)} %bitcast.1), custom_call_target="tpu_custom_call" | custom-call | tf_op jit(solution)/shard_map/pallas_call | solution.py:300
  45.7 1.5 %copy.4 = f32[128,128]{1,0:T(8,128)} copy(f32[128,128]{1,0:T(8,128)} %shard_map.28) | data formatting | bytes 131072

commit v4 on v3

--- a/solution.py
+++ b/solution.py
@@ -91,12 +91,16 @@
     partner = col_of(q, 1 - b)
     group = 2 if R % 2 == 0 else 1
     groups = [list(range(g, g + group)) for g in range(0, R, group)]
-    near_first = [1] + list(range(R - 1, 1, -1)) if R > 1 else []
+    row_order = [t for t in range(2, R)] + [t for t in range(1, min(R, 2))]
+    chip_order = list(range(Q - 1, 0, -1))
+
+    def bits(size):
+        return [1 << i for i in range(size.bit_length() - 1)]
 
     barrier = pltpu.get_barrier_semaphore()
-    for t in range(1, R):
+    for t in bits(R):
         pl.semaphore_signal(barrier, inc=1, device_id=(row_peer(t), c), device_id_type=MESH)
-    for u in range(1, C):
+    for u in bits(C):
         pl.semaphore_signal(barrier, inc=1, device_id=(r, flip(c, u, C)), device_id_type=MESH)
 
     def ready_column(x, t):
@@ -115,35 +119,66 @@
     m1[block(0), :] = own_member.astype(jnp.bfloat16)
     ready_column(e_ref[...], 0)
 
-    pl.semaphore_wait(barrier, R + C - 2)
-
-    seeds_col = {}
-    for s in range(Q):
-        for o in range(2):
-            if s or o:
-                seeds_col[s, o] = send(
-                    s_ref, s_row.at[2 * s + b], sr_s.at[2 * s + o], sr_r.at[2 * s + o],
-                    r, col_of(chip_peer(s), (b + o) % 2),
-                )
-    seeds_rw = {}
+    pl.semaphore_wait(barrier, len(bits(R)) + len(bits(C)))
+
+    seeds_col, seeds_rw, direct, alongz = {}, {}, {}, {}
+
+    def send_seeds_col(u):
+        seeds_col[u] = send(
+            s_ref, s_row.at[(u // 2) * 2 + b], sr_s.at[u], sr_r.at[u], r, flip(c, u, C)
+        )
+
+    def send_seeds_rw(t):
+        seeds_rw[t] = send(s_ref, s_col.at[t], sc_s.at[t], sc_r.at[t], row_peer(t), c)
+
+    def send_alongz(t):
+        alongz[t] = send(e_ref, e_col.at[block(t)], ec_s.at[t], ec_r.at[t], row_peer(t), c)
+
+    def send_direct(s):
+        direct[s] = send(
+            e_ref, e_row.at[row_slot(s, b)], er_s.at[s], er_r.at[s], r,
+            partner if s == 0 else col_of(chip_peer(s), b),
+        )
+
+    for t in bits(R):
+        send_seeds_rw(t)
+    for u in bits(C):
+        send_seeds_col(u)
+    far_rows, far_chips = bits(R)[::-1], bits(C)[:0:-1]
+    for i in range(max(len(far_rows), len(far_chips))):
+        if i < len(far_rows):
+            send_alongz(far_rows[i])
+        if i < len(far_chips):
+            send_direct(far_chips[i] // 2)
+    send_direct(0)
+
+    heard_row, heard_col = set(), set()
     for t in range(1, R):
-        seeds_rw[t] = send(s_ref, s_col.at[t], sc_s.at[t], sc_r.at[t], row_peer(t), c)
-
-    direct, alongz = {}, {}
-    for t in near_first:
-        alongz[t] = send(e_ref, e_col.at[block(t)], ec_s.at[t], ec_r.at[t], row_peer(t), c)
-    for s in range(Q - 1, 0, -1):
-        direct[s] = send(
-            e_ref, e_row.at[row_slot(s, b)], er_s.at[s], er_r.at[s], r, col_of(chip_peer(s), b)
-        )
-    direct[0] = send(e_ref, e_row.at[row_slot(0, b)], er_s.at[0], er_r.at[0], r, partner)
-
-    for s, o in seeds_col:
-        seeds_col[s, o].wait_recv()
-        core = (b + o) % 2
-        m_row[row_slot(s, core), :] = seeds_to_member(s_row[2 * s + core])
+        if t not in bits(R):
+            via = t - (1 << (t.bit_length() - 1))
+            if via not in heard_row:
+                seeds_rw[via].wait_recv()
+                heard_row.add(via)
+            send_seeds_rw(t)
+            send_alongz(t)
+    for u in range(1, C):
+        if u not in bits(C):
+            via = u - (1 << (u.bit_length() - 1))
+            if via not in heard_col:
+                seeds_col[via].wait_recv()
+                heard_col.add(via)
+            send_seeds_col(u)
+            if u % 2 == 0:
+                send_direct(u // 2)
+
+    for u in range(1, C):
+        if u not in heard_col:
+            seeds_col[u].wait_recv()
+        core = (b + u) % 2
+        m_row[row_slot(u // 2, core), :] = seeds_to_member(s_row[(u // 2) * 2 + core])
     for t in range(1, R):
-        seeds_rw[t].wait_recv()
+        if t not in heard_row:
+            seeds_rw[t].wait_recv()
         m1[block(t), :] = seeds_to_member(s_col[t]).astype(jnp.bfloat16)
 
     relay = {}
@@ -267,12 +302,16 @@
         if w + 1 < SWEEPS:
             own_member = jnp.exp(log_member)
             m_own[...] = own_member
-            for t in near_first:
-                mz[t] = send(m_own, m_col.at[block(t)], mz_s.at[t], mz_r.at[t], row_peer(t), c)
-            for s in range(Q - 1, 0, -1):
-                mc[s] = send(
-                    m_own, m_row.at[row_slot(s, b)], mc_s.at[s], mc_r.at[s], r, col_of(chip_peer(s), b)
-                )
+            for i in range(max(R, Q) - 1):
+                if i < R - 1:
+                    t = row_order[i]
+                    mz[t] = send(m_own, m_col.at[block(t)], mz_s.at[t], mz_r.at[t], row_peer(t), c)
+                if i < Q - 1:
+                    s = chip_order[i]
+                    mc[s] = send(
+                        m_own, m_row.at[row_slot(s, b)], mc_s.at[s], mc_r.at[s],
+                        r, col_of(chip_peer(s), b),
+                    )
             mc[0] = send(m_own, m_row.at[row_slot(0, b)], mc_s.at[0], mc_r.at[0], r, partner)
             m_row[row_slot(0, b), :] = own_member
 

time: 47.3 us -> 46.9 us (level)
  Pallas kernels: 45.7 us -> 45.2 us
    pallas_call x1, Pallas kernels: 45.7 us -> 45.2 us  [shards(): pl.pallas_call(functools.partial(kernel, R, C), out_shape=jax.ShapeDtypeS...]
where the time goes in v4:
time: 46.9 us; the launch traced here: 46.7 us
  Pallas kernels  45.2 us (96%)
  local copies, waits for them, and re-layouts  1.47 us (3%)
    pallas_call x1, Pallas kernels, shards(): pl.pallas_call(functools.partial(kernel, R, C), out_shape=jax.ShapeDtypeS...  45.2 us
    unnamed x1, local copies, waits for them, and re-layouts  1.47 us

profile of v4, /device:TPU:0, one launch (start us, length us, event | category | flops | bytes accessed | tf_op | source)
XLA Modules:
  0.0 46.7 jit_solution(13915489282817694062)
XLA Ops:
  0.0 45.2 %shard_map.28 = f32[128,128]{1,0:T(8,128)} custom-call(f32[128,256]{1,0:T(8,128)} %e_ref.1, s32[1,128]{1,0:T(1,128)} %bitcast.1), custom_call_target="tpu_custom_call" | custom-call | tf_op jit(solution)/shard_map/pallas_call | solution.py:339
  45.2 1.5 %copy.4 = f32[128,128]{1,0:T(8,128)} copy(f32[128,128]{1,0:T(8,128)} %shard_map.28) | data formatting | bytes 131072

commit v5 on v4

--- a/solution.py
+++ b/solution.py
@@ -82,6 +82,9 @@
     def block(i):
         return pl.ds(i * n, n) if isinstance(i, int) else pl.ds(pl.multiple_of(i * n, n), n)
 
+    def column_slot(t):
+        return block(arrival.index(t))
+
     def row_slot(s, core):
         return block(2 * s + core)
 
@@ -90,8 +93,10 @@
 
     partner = col_of(q, 1 - b)
     group = 2 if R % 2 == 0 else 1
-    groups = [list(range(g, g + group)) for g in range(0, R, group)]
-    row_order = [t for t in range(2, R)] + [t for t in range(1, min(R, 2))]
+    near = [1 << i for i in range(R.bit_length() - 1)]
+    arrival = [0] + near[::-1] + [t for t in range(1, R) if t not in near]
+    groups = [arrival[g : g + group] for g in range(0, R, group)]
+    row_order = arrival[1:]
     chip_order = list(range(Q - 1, 0, -1))
 
     def bits(size):
@@ -104,7 +109,7 @@
         pl.semaphore_signal(barrier, inc=1, device_id=(r, flip(c, u, C)), device_id_type=MESH)
 
     def ready_column(x, t):
-        at = block(t)
+        at = column_slot(t)
         p1, p2, p3 = split3(x)
         c1[at, :] = p1
         c2[at, :] = p2
@@ -132,7 +137,7 @@
         seeds_rw[t] = send(s_ref, s_col.at[t], sc_s.at[t], sc_r.at[t], row_peer(t), c)
 
     def send_alongz(t):
-        alongz[t] = send(e_ref, e_col.at[block(t)], ec_s.at[t], ec_r.at[t], row_peer(t), c)
+        alongz[t] = send(e_ref, e_col.at[column_slot(t)], ec_s.at[t], ec_r.at[t], row_peer(t), c)
 
     def send_direct(s):
         direct[s] = send(
@@ -179,7 +184,7 @@
     for t in range(1, R):
         if t not in heard_row:
             seeds_rw[t].wait_recv()
-        m1[block(t), :] = seeds_to_member(s_col[t]).astype(jnp.bfloat16)
+        m1[column_slot(t), :] = seeds_to_member(s_col[t]).astype(jnp.bfloat16)
 
     relay = {}
     for s in range(1, Q):
@@ -188,7 +193,7 @@
         relay[s] = send(e_row.at[at], e_row.at[at], rel_s.at[s], rel_r.at[s], r, partner)
 
     def span(ts):
-        return pl.ds(ts[0] * n, len(ts) * n)
+        return pl.ds(arrival.index(ts[0]) * n, len(ts) * n)
 
     def make_distance(s, ts):
         pair, cols = pair_slot(s), span(ts)
@@ -233,15 +238,15 @@
         products = make_distance if w == 0 else take_distance
         last = None
         for at, ts in enumerate(groups):
-            for t in sorted(ts, reverse=True):
+            for t in ts:
                 if t == 0:
                     continue
                 if w == 0:
                     alongz[t].wait_recv()
-                    ready_column(e_col[block(t), :], t)
+                    ready_column(e_col[column_slot(t), :], t)
                 else:
                     mz[t].wait_recv()
-                    ready_member(m_col[block(t), :], t)
+                    ready_member(m_col[column_slot(t), :], t)
             final = at + 1 == len(groups)
             for s in (range(Q) if at == 0 else order):
                 if at == 0 and w == 0:
@@ -305,7 +310,7 @@
             for i in range(max(R, Q) - 1):
                 if i < R - 1:
                     t = row_order[i]
-                    mz[t] = send(m_own, m_col.at[block(t)], mz_s.at[t], mz_r.at[t], row_peer(t), c)
+                    mz[t] = send(m_own, m_col.at[column_slot(t)], mz_s.at[t], mz_r.at[t], row_peer(t), c)
                 if i < Q - 1:
                     s = chip_order[i]
                     mc[s] = send(
@@ -316,7 +321,7 @@
             m_row[row_slot(0, b), :] = own_member
 
             def ready_member(x, t):
-                at = block(t)
+                at = column_slot(t)
                 p1, p2, p3 = split3(x)
                 m1[at, :] = p1
                 m2[at, :] = p2

time: 46.9 us -> 47.6 us (1.015)
  Pallas kernels: 45.2 us -> 45.9 us
    pallas_call x1, Pallas kernels: 45.2 us -> 45.9 us  [shards(): pl.pallas_call(functools.partial(kernel, R, C), out_shape=jax.ShapeDtypeS...]
where the time goes in v5:
time: 47.6 us; the launch traced here: 47.4 us
  Pallas kernels  45.9 us (96%)
  local copies, waits for them, and re-layouts  1.47 us (3%)
    pallas_call x1, Pallas kernels, shards(): pl.pallas_call(functools.partial(kernel, R, C), out_shape=jax.ShapeDtypeS...  45.9 us
    unnamed x1, local copies, waits for them, and re-layouts  1.47 us

profile of v5, /device:TPU:0, one launch (start us, length us, event | category | flops | bytes accessed | tf_op | source)
XLA Modules:
  0.0 47.4 jit_solution(10739751367828969012)
XLA Ops:
  0.0 45.9 %shard_map.28 = f32[128,128]{1,0:T(8,128)} custom-call(f32[128,256]{1,0:T(8,128)} %e_ref.1, s32[1,128]{1,0:T(1,128)} %bitcast.1), custom_call_target="tpu_custom_call" | custom-call | tf_op jit(solution)/shard_map/pallas_call | solution.py:344
  45.9 1.5 %copy.4 = f32[128,128]{1,0:T(8,128)} copy(f32[128,128]{1,0:T(8,128)} %shard_map.28) | data formatting | bytes 131072
